TPU v7x, 256 devices: a whole 4x4x8 slice. The times are simulated.
256 devices in a mesh: expert: 8 (over x, core), dp: 8 (over z), pipe: 4 (over y).
Axes of the slice: x: 4, y: 4, z: 8, core: 2. Of those that a mesh axis runs over, the one named last changes fastest.
Arguments:
- tokens: bfloat16 [2048, 3072], P(('expert', 'dp'), 'pipe'), may hold values from -6 to 6
- out_grad: bfloat16 [2048, 3072], P(('expert', 'dp'), 'pipe'), may hold values from -6 to 6
- gate_values: float32 [2048, 2], P(('expert', 'dp')), may hold values from 0.1 to 1
- expert_ids: int32 [2048, 2], P(('expert', 'dp')), may hold values from 0 to 7, all different within a row; in each aligned block of 32 rows (0 to 31, 32 to 63, ...) at most 16 rows name the same one
- w_gate: bfloat16 [8, 3072, 8192], P('expert', None, ('dp', 'pipe')), may hold values from -0.109375 to 0.109375
- w_up: bfloat16 [8, 3072, 8192], P('expert', None, ('dp', 'pipe')), may hold values from -0.109375 to 0.109375
- w_down: bfloat16 [8, 8192, 3072], P('expert', ('dp', 'pipe')), may hold values from -0.0625 to 0.0625
Outputs:
- grad_tokens: bfloat16 [2048, 3072], P(('expert', 'dp'), 'pipe')
- gate_weight_gradient: bfloat16 [8, 3072, 8192], P('expert', None, ('dp', 'pipe'))
- up_weight_gradient: bfloat16 [8, 3072, 8192], P('expert', None, ('dp', 'pipe'))
- grad_down: bfloat16 [8, 8192, 3072], P('expert', ('dp', 'pipe'))
Inputs may be any that keep to these rules, and one draw needn't show every extreme that they name: `expert_ids`: each token names two different experts; among the 32 tokens of one block no expert is named more than 16 times, and in some blocks one is named exactly 16 times.
All inputs are finite; a program needn't handle non-finite values.
Results may differ from a plain program's by a relative error of at most 0.0065.
Values may be sent and summed in bfloat16 or wider, within the bound.
No kernel may reach another device: no remote copies, remote signals or barrier semaphores. Data moves between devices by JAX's collectives and lax.ppermute only.
A program may use at most 128 MiB of HBM per device.

v0:
```python
import jax
import jax.numpy as jnp
from jax import lax
from jax.sharding import PartitionSpec as P


def dispatch_tables(expert_ids, gate_values, expert_count, capacity):
    token_count = expert_ids.shape[0]
    choices_flat = expert_ids.reshape(-1)
    one_hot = (choices_flat[:, None] == jnp.arange(expert_count, dtype=jnp.int32)[None, :]).astype(
        jnp.int32
    )
    ranks = jnp.cumsum(one_hot, axis=0) - 1
    slot_index = choices_flat * capacity + jnp.sum(one_hot * ranks, axis=1)
    hits = jnp.arange(expert_count * capacity, dtype=jnp.int32)[:, None] == slot_index[None, :]
    hits = hits.reshape(expert_count * capacity, token_count, 2)
    picker = jnp.any(hits, axis=2).astype(jnp.bfloat16)
    weighting = jnp.sum(jnp.where(hits, gate_values[None, :, :], 0.0), axis=2)
    return (picker, weighting)


def fill_slots(picker, weighting, features, cotangent):
    sent_rows = jnp.dot(picker, features, preferred_element_type=jnp.float32).astype(jnp.bfloat16)
    sent_grads = jnp.dot(
        weighting, cotangent.astype(jnp.float32), precision=lax.Precision.HIGHEST
    ).astype(jnp.bfloat16)
    return (sent_rows, sent_grads)


def body(tokens, out_grad, gate_values, expert_ids, w_gate, w_up, w_down):
    expert_count = lax.axis_size("expert")
    group_count = lax.axis_size("dp")
    pipe_count = lax.axis_size("pipe")
    token_count = tokens.shape[0]
    capacity = max(token_count // 2, 2 * token_count // expert_count)
    slot_total = expert_count * capacity
    feat_part = tokens.shape[1]
    model_width = feat_part * pipe_count
    hidden_part = w_gate.shape[2]
    picker, weighting = dispatch_tables(expert_ids, gate_values, expert_count, capacity)
    sent_rows, sent_grads = fill_slots(picker, weighting, tokens, out_grad)
    recv_rows, recv_grads = (
        lax.all_to_all(
            sent_rows.reshape(expert_count, capacity, feat_part),
            "expert",
            split_axis=0,
            concat_axis=0,
            tiled=True,
        ),
        lax.all_to_all(
            sent_grads.reshape(expert_count, capacity, feat_part),
            "expert",
            split_axis=0,
            concat_axis=0,
            tiled=True,
        ),
    )
    gathered_rows, gathered_gradients = (
        lax.all_gather(
            recv_rows.reshape(1, slot_total, feat_part), ("dp", "pipe"), axis=0, tiled=True
        ),
        lax.all_gather(
            recv_grads.reshape(1, slot_total, feat_part), ("dp", "pipe"), axis=0, tiled=True
        ),
    )
    piece_width = model_width // pipe_count
    gathered_rows = gathered_rows.reshape(group_count, pipe_count, slot_total, piece_width)
    gathered_gradients = gathered_gradients.reshape(
        group_count, pipe_count, slot_total, piece_width
    )
    gate_weight_blocks = w_gate[0].reshape(pipe_count, piece_width, hidden_part)
    up_weight_blocks = w_up[0].reshape(pipe_count, piece_width, hidden_part)
    down_weight_blocks = w_down[0].reshape(hidden_part, pipe_count, piece_width)
    gate_pre = jnp.einsum(
        "lxvk,xkh->lvh", gathered_rows, gate_weight_blocks, preferred_element_type=jnp.float32
    )
    up_preactivation = jnp.einsum(
        "lxvk,xkh->lvh", gathered_rows, up_weight_blocks, preferred_element_type=jnp.float32
    )
    act_grad = jnp.einsum(
        "mzyj,uzj->myu", gathered_gradients, down_weight_blocks, preferred_element_type=jnp.float32
    )
    sigmoid_gate = jax.nn.sigmoid(gate_pre)
    linear = gate_pre * sigmoid_gate
    swiglu_activation = (linear * up_preactivation).astype(jnp.bfloat16)
    slope_term = sigmoid_gate * (1.0 + gate_pre * (1.0 - sigmoid_gate))
    gate_output_gradient = (act_grad * up_preactivation * slope_term).astype(jnp.bfloat16)
    up_output_gradient = (act_grad * linear).astype(jnp.bfloat16)
    gate_weight_gradient = jnp.einsum(
        "kctx,ktn->cxn", gathered_rows, gate_output_gradient, preferred_element_type=jnp.float32
    )
    gate_weight_gradient = gate_weight_gradient.reshape(model_width, hidden_part).astype(
        jnp.bfloat16
    )[None]
    up_weight_gradient = jnp.einsum(
        "kctx,ktn->cxn", gathered_rows, up_output_gradient, preferred_element_type=jnp.float32
    )
    up_weight_gradient = up_weight_gradient.reshape(model_width, hidden_part).astype(jnp.bfloat16)[
        None
    ]
    grad_down = jnp.einsum(
        "cjb,cvji->bvi", swiglu_activation, gathered_gradients, preferred_element_type=jnp.float32
    )
    grad_down = grad_down.reshape(hidden_part, model_width).astype(jnp.bfloat16)[None]
    gate_backward = w_gate[0].reshape(pipe_count, feat_part, hidden_part)
    up_backward = w_up[0].reshape(pipe_count, feat_part, hidden_part)
    input_terms = jnp.einsum(
        "mil,xkl->mxik", gate_output_gradient, gate_backward, preferred_element_type=jnp.float32
    ) + jnp.einsum(
        "mil,xkl->mxik", up_output_gradient, up_backward, preferred_element_type=jnp.float32
    )
    summed = lax.psum_scatter(
        input_terms.reshape(group_count * pipe_count, slot_total, feat_part),
        ("dp", "pipe"),
        scatter_dimension=0,
        tiled=True,
    )
    slot_grads = summed.astype(jnp.bfloat16).reshape(expert_count, capacity, feat_part)
    returned = lax.all_to_all(slot_grads, "expert", split_axis=0, concat_axis=0, tiled=True)
    grad_tokens = jnp.einsum(
        "st,sq->tq",
        picker,
        returned.reshape(slot_total, feat_part),
        preferred_element_type=jnp.float32,
    ).astype(jnp.bfloat16)
    return (grad_tokens, gate_weight_gradient, up_weight_gradient, grad_down)


def solution(mesh):
    placed = (
        P(("expert", "dp"), "pipe"),
        P(("expert", "dp"), "pipe"),
        P(("expert", "dp"), None),
        P(("expert", "dp"), None),
        P("expert", None, ("dp", "pipe")),
        P("expert", None, ("dp", "pipe")),
        P("expert", ("dp", "pipe"), None),
    )
    return jax.shard_map(
        body,
        mesh=mesh,
        in_specs=placed,
        out_specs=(
            P(("expert", "dp"), "pipe"),
            P("expert", None, ("dp", "pipe")),
            P("expert", None, ("dp", "pipe")),
            P("expert", ("dp", "pipe"), None),
        ),
        check_vma=False,
    )
```

profile of v0, /device:TPU:1, one launch (start us, length us, event | category | flops | bytes accessed | tf_op | source)
XLA Modules:
  0.0 471.8 jit_solution(10820452683716536585)
XLA Ops:
  7.2 0.9 copy.50
  8.1 0.1 eq.30
  8.2 0.1 fusion.17
  8.3 0.1 reduce_window_sum.11
  8.4 0.2 select_reduce_fusion.1
  8.6 0.1 reduce_sum.21
  8.7 0.1 copy.51
  8.8 0.7 multiply_add_fusion
  9.4 0.1 fusion.18
  9.5 1.1 convolution_convert_fusion
  10.6 12.1 %all_to_all.15 = bf16[8,16,768]{2,1,0:T(8,128)(2,1)} all-to-all(bf16[8,16,768]{2,1,0:T(8,128)(2,1)S(1)} %bitcast.111), channel_id=1, replica_groups=mesh['expert'=8,'dp'=8,'pipe'=4] {'expert'}, dimensions={0} | all-to-all | bytes 393216 | tf_op jit(solution)/shard_map/all_to_all | solution.py:43
  22.8 0.8 select_reduce_fusion
  23.5 1.2 convolution_convert_fusion.1
  24.7 9.9 %all_to_all.16 = bf16[8,16,768]{2,1,0:T(8,128)(2,1)} all-to-all(bf16[8,16,768]{2,1,0:T(8,128)(2,1)S(1)} %bitcast.110), channel_id=1, replica_groups=mesh['expert'=8,'dp'=8,'pipe'=4] {'expert'}, dimensions={0} | all-to-all | bytes 393216 | tf_op jit(solution)/shard_map/all_to_all | solution.py:50
  34.6 0.0 reduce-scatter.2.cloned.1.call-start
  34.7 3.3 reshape_squeeze.11
  38.0 73.0 %all-gather.5.cloned.1.call-done = bf16[32,128,768]{2,1,0:T(8,128)(2,1)} async-done(((bf16[1,128,768]{2,1,0:T(8,128)(2,1)}), bf16[32,128,768]{2,1,0:T(8,128)(2,1)}) %all-gather.5.cloned.1.call-update) | async-done | bytes 6291472 | tf_op jit(solution)/shard_map/all_gather | solution.py:59
  111.0 5.7 %convolution_bitcast_fusion.3 = f32[8,128,256]{2,1,0:T(8,128)} fusion(bf16[8,4,128,768]{3,2,1,0:T(8,128)(2,1)} %bitcast.97, bf16[4,768,256,1]{2,1,0,3:T(8,128)(2,1)S(1)} %bitcast.94), kind=kOutput, calls=%fused_computation.14 | convolution fusion | flops 1610612736 | bytes 8912896 | tf_op jit(solution)/shard_map/lxvk,xkh->lvh/dot_general | solution.py:74
  116.7 2.8 convolution_bitcast_fusion.4
  119.4 79.2 %all-gather.3.cloned.1.call-done = bf16[32,128,768]{2,1,0:T(8,128)(2,1)} async-done(((bf16[1,128,768]{2,1,0:T(8,128)(2,1)}), bf16[32,128,768]{2,1,0:T(8,128)(2,1)}) %all-gather.3.cloned.1.call-update) | async-done | bytes 6291472 | tf_op jit(solution)/shard_map/all_gather | solution.py:62
  198.7 5.4 %multiply_convert_fusion.1 = (bf16[8,128,256]{2,1,0:T(8,128)(2,1)S(1)}, bf16[8,128,256]{2,1,0:T(8,128)(2,1)S(1)}) fusion(f32[8,128,256]{2,1,0:T(8,128)} %convolution_bitcast_fusion.3, f32[8,128,256]{2,1,0:T(8,128)} %convolution_bitcast_fusion.4, bf16[8,4,128,768]{3,2,1,0:T(8,128)(2,1)} %bitcast.100, bf16[256,4,768]{2,1,0:T(4,128)(2,1)S(1)} %reshape_squeeze.11), kind=kOutput, calls=%fused_computation.20 | convolution fusion | flops 1614020608 | bytes 11010048 | tf_op jit(solution)/shard_map/mzyj,uzj->myu/dot_general | solution.py:80
  204.1 1.8 fusion.14
  206.0 6.4 %convolution_add_fusion = f32[8,128,4,768]{3,1,2,0:T(8,128)} fusion(f32[8,128,4,768]{3,1,2,0:T(8,128)S(1)} %fusion.14, bf16[4,768,256,1]{2,1,0,3:T(8,128)(2,1)S(1)} %bitcast.106, bf16[8,128,256]{2,1,0:T(8,128)(2,1)S(1)} %get-tuple-element.4), kind=kOutput, calls=%fused_computation | convolution fusion | flops 1613758464 | bytes 27262976 | tf_op jit(solution)/shard_map/mil,xkl->mxik/dot_general | solution.py:109
  212.3 8.6 %copy.65 = bf16[4,768,8,128]{3,1,0,2:T(8,128)(2,1)} copy(bf16[4,768,8,128]{1,3,0,2:T(8,128)(2,1)} %bitcast.98) | data formatting | bytes 12582912 | tf_op jit(solution)/shard_map/kctx,ktn->cxn/dot_general | solution.py:89
  220.9 8.8 %copy.67 = bf16[4,768,8,128]{3,1,0,2:T(8,128)(2,1)} copy(bf16[4,768,8,128]{1,3,0,2:T(8,128)(2,1)} %bitcast.101) | data formatting | bytes 12582912 | tf_op jit(solution)/shard_map/cjb,cvji->bvi/dot_general | solution.py:101
  229.7 7.5 %fusion.4 = bf16[1,3072,256]{2,1,0:T(8,128)(2,1)} fusion(bf16[3072,8,128]{2,0,1:T(8,128)(2,1)} %bitcast.102, bf16[8,128,256]{2,1,0:T(8,128)(2,1)S(1)} %copy-done.8), kind=kOutput, calls=%fused_computation.8 | convolution fusion | flops 1611399168 | bytes 8388608 | tf_op jit(solution)/shard_map/kctx,ktn->cxn/dot_general | solution.py:95
  237.2 3.1 fusion.3
  240.3 206.2 %reduce-scatter.2.cloned.1.call-done = f32[1,128,768]{2,1,0:T(8,128)} async-done(((f32[32,128,768]{2,1,0:T(8,128)}), f32[1,128,768]{2,1,0:T(8,128)}) %reduce-scatter.2.cloned.1.call-update) | async-done | bytes 393232 | tf_op jit(solution)/shard_map/reduce_scatter | solution.py:112
  446.5 1.7 convert_element_type.40
  448.2 9.1 %all-to-all-start.2 = ((bf16[8,16,768]{2,1,0:T(8,128)(2,1)}), bf16[8,16,768]{2,1,0:T(8,128)(2,1)S(1)}, u32[]{:S(2)}, u32[]{:S(2)}) async-start(bf16[8,16,768]{2,1,0:T(8,128)(2,1)} %bitcast.24), calls=%async_computation.3 | async-start | bytes 393216 | tf_op jit(solution)/shard_map/all_to_all | solution.py:119
  457.3 7.3 %fusion.5 = bf16[1,3072,256]{2,1,0:T(8,128)(2,1)} fusion(bf16[3072,8,128]{2,0,1:T(8,128)(2,1)} %bitcast.103, bf16[8,128,256]{2,1,0:T(8,128)(2,1)S(1)} %copy-done.6), kind=kOutput, calls=%fused_computation.9 | convolution fusion | flops 1611399168 | bytes 8388608 | tf_op jit(solution)/shard_map/kctx,ktn->cxn/dot_general | solution.py:89
  464.5 0.8 convolution_convert_fusion.2
  (28 shorter events, 0.2 us)
Async XLA Ops:
  7.2 103.8 %copy-start = (bf16[1,3072,256]{2,1,0:T(8,128)(2,1)S(1)}, bf16[1,3072,256]{2,1,0:T(8,128)(2,1)}, u32[]{:S(2)}) copy-start(bf16[1,3072,256]{2,1,0:T(8,128)(2,1)} %param.11) | copy-start | bytes 4718596
  7.2 103.8 %all-gather.5.cloned.1.call-start = ((), (), s32[]{:S(2)}) async-start(), calls=%async_computation.5 | async-start | bytes 6488064 | tf_op jit(solution)/shard_map/all_gather | solution.py:59
  22.7 176.0 %all-gather.3.cloned.1.call-start = ((), (), s32[]{:S(2)}) async-start(), calls=%async_computation.4 | async-start | bytes 6488064 | tf_op jit(solution)/shard_map/all_gather | solution.py:62
  34.6 411.9 %reduce-scatter.2.cloned.1.call-start = ((), (), s32[]{:S(2)}) async-start(), calls=%async_computation.6 | async-start | bytes 12976128 | tf_op jit(solution)/shard_map/reduce_scatter | solution.py:112
  111.0 5.7 %copy-start.1 = (bf16[32,128,768]{2,1,0:T(8,128)(2,1)S(1)}, bf16[32,128,768]{2,1,0:T(8,128)(2,1)}, u32[]{:S(2)}) copy-start(bf16[32,128,768]{2,1,0:T(8,128)(2,1)} %all-gather.5.cloned.1.call-done) | copy-start | bytes 18874372
  111.0 5.7 %copy-start.3 = (bf16[1,3072,256]{2,1,0:T(8,128)(2,1)S(1)}, bf16[1,3072,256]{2,1,0:T(8,128)(2,1)}, u32[]{:S(2)}) copy-start(bf16[1,3072,256]{2,1,0:T(8,128)(2,1)} %param.12) | copy-start | bytes 4718596
  204.1 1.9 copy-start.5
  204.1 1.9 copy-start.7
  204.1 1.9 copy-start.4
  220.9 8.8 %copy-start.8 = (bf16[8,128,256]{2,1,0:T(8,128)(2,1)S(1)}, bf16[8,128,256]{2,1,0:T(8,128)(2,1)}, u32[]{:S(2)}) copy-start(bf16[8,128,256]{2,1,0:T(8,128)(2,1)} %copy-done.7) | copy-start | bytes 1572868
  229.7 7.5 %copy-start.2 = (bf16[4,768,8,128]{3,1,0,2:T(8,128)(2,1)S(1)}, bf16[4,768,8,128]{3,1,0,2:T(8,128)(2,1)}, u32[]{:S(2)}) copy-start(bf16[4,768,8,128]{3,1,0,2:T(8,128)(2,1)} %copy.67) | copy-start | bytes 18874372
  229.7 7.5 %copy-start.9 = (f32[8,128,256]{2,1,0:T(8,128)S(1)}, f32[8,128,256]{2,1,0:T(8,128)}, u32[]{:S(2)}) copy-start(f32[8,128,256]{2,1,0:T(8,128)} %convolution_bitcast_fusion.3) | copy-start | bytes 3145732
  229.7 7.5 %copy-start.10 = (f32[8,128,256]{2,1,0:T(8,128)S(1)}, f32[8,128,256]{2,1,0:T(8,128)}, u32[]{:S(2)}) copy-start(f32[8,128,256]{2,1,0:T(8,128)} %convolution_bitcast_fusion.4) | copy-start | bytes 3145732
  237.2 220.1 %copy-start.6 = (bf16[8,128,256]{2,1,0:T(8,128)(2,1)S(1)}, bf16[8,128,256]{2,1,0:T(8,128)(2,1)}, u32[]{:S(2)}) copy-start(bf16[8,128,256]{2,1,0:T(8,128)(2,1)} %copy-done.5) | copy-start | bytes 1572868
  448.2 16.3 %all-to-all-start.2 = ((bf16[8,16,768]{2,1,0:T(8,128)(2,1)}), bf16[8,16,768]{2,1,0:T(8,128)(2,1)S(1)}, u32[]{:S(2)}, u32[]{:S(2)}) async-start(bf16[8,16,768]{2,1,0:T(8,128)(2,1)} %bitcast.24), calls=%async_computation.3 | async-start | bytes 393216 | tf_op jit(solution)/shard_map/all_to_all | solution.py:119
Sparse Core Ops, SparseCore 0:
  22.9 88.0 all-gather.4
  113.6 85.0 all-gather.2
  212.5 233.9 reduce-scatter.1
where the time goes:
time: 473 us; the launch traced here: 472 us
  waiting for transfers between devices  359 us (76%)
  matrix products  42.8 us (9%)
  blocking collectives  22 us (5%)
  local copies, waits for them, and re-layouts  21.8 us (5%)
  between operations  13.9 us (3%)
  starting transfers between devices  9.19 us (2%)
    reduce_scatter x1, waiting for transfers between devices, body(): lax.psum_scatter(input_terms.reshape(group_count * pipe_count, slot_total...  206 us
    all_gather x1, waiting for transfers between devices, body(): lax.all_gather(recv_grads.reshape(1, slot_total, feat_part), ('dp', 'pipe...  79.2 us
    all_gather x1, waiting for transfers between devices, body(): lax.all_gather(recv_rows.reshape(1, slot_total, feat_part), ('dp', 'pipe'...  73 us
    all_to_all x1, blocking collectives, body(): lax.all_to_all(sent_rows.reshape(expert_count, capacity, feat_part), 'exp...  12.1 us
    all_to_all x1, blocking collectives, body(): lax.all_to_all(sent_grads.reshape(expert_count, capacity, feat_part), 'ex...  9.87 us
  transfers between devices with their start and end apart: 4, of which 3 were waited for; matrix products, arithmetic and copies ran while one was open for 10% of the time, Pallas kernels for 0%

commit v1 on v0

v1 whole, which is shorter than its diff:
```python
import functools

import jax
import jax.numpy as jnp
from jax import lax
from jax.experimental import pallas as pl
from jax.experimental.pallas import tpu as pltpu
from jax.sharding import PartitionSpec as P

F32 = jnp.float32
BF16 = jnp.bfloat16
INTERPRET = False
VMEM_LIMIT = 58 * 1024 * 1024
NN = (((1,), (0,)), ((), ()))
NT = (((1,), (1,)), ((), ()))


def dot(a, b, dims=NN):
    return lax.dot_general(a, b, dims, preferred_element_type=F32)


def slot_indices(expert_ids, expert_count, capacity):
    choices_flat = expert_ids.reshape(-1)
    one_hot = (choices_flat[:, None] == jnp.arange(expert_count, dtype=jnp.int32)[None, :]).astype(
        jnp.int32
    )
    ranks = jnp.cumsum(one_hot, axis=0) - 1
    return (choices_flat * capacity + jnp.sum(one_hot * ranks, axis=1)).reshape(-1, 2)


def fill_slots(slot_index, gate_values, slot_total, features, cotangent):
    hits = jnp.arange(slot_total, dtype=jnp.int32)[:, None, None] == slot_index[None, :, :]
    picker = jnp.any(hits, axis=2).astype(BF16)
    weighting = jnp.sum(jnp.where(hits, gate_values[None, :, :], 0.0), axis=2)
    sent_rows = jnp.dot(picker, features, preferred_element_type=F32).astype(BF16)
    sent_grads = jnp.dot(weighting, cotangent.astype(F32), precision=lax.Precision.HIGHEST).astype(
        BF16
    )
    return (picker, sent_rows, sent_grads)


def expert_kernel(expert_count, x_ref, wg_ref, wu_ref, wd_ref, act_ref, gg_ref, ug_ref, ring_ref, cross_ref):
    groups, pipes, both, feat = x_ref.shape
    rows = both // 2
    total = groups * rows
    half = feat // 2
    capacity = rows // expert_count
    gate = up = act_grad = None
    for p in range(pipes):
        features = x_ref[:, p, :rows, :].reshape(total, feat)
        cotangent = x_ref[:, p, rows:, :].reshape(total, feat)
        cols = slice(p * feat, (p + 1) * feat)
        g = dot(features, wg_ref[cols, :])
        u = dot(features, wu_ref[cols, :])
        a = dot(cotangent, wd_ref[:, cols], NT)
        gate = g if gate is None else gate + g
        up = u if up is None else up + u
        act_grad = a if act_grad is None else act_grad + a
    sig = jax.nn.sigmoid(gate)
    linear = gate * sig
    act = (linear * up).astype(BF16)
    gate_grad = (act_grad * up * (sig * (1.0 + gate * (1.0 - sig)))).astype(BF16)
    up_grad = (act_grad * linear).astype(BF16)
    act_ref[...] = act.T
    gg_ref[...] = gate_grad.T
    ug_ref[...] = up_grad.T
    for p in range(pipes):
        cols = slice(p * feat, (p + 1) * feat)
        back = (dot(gate_grad, wg_ref[cols, :], NT) + dot(up_grad, wu_ref[cols, :], NT)).astype(BF16)
        ring_ref[p] = back[:, :half]
        for d in range(groups):
            part = back[d * rows : (d + 1) * rows, half:]
            cross_ref[:, p, d * capacity : (d + 1) * capacity, :] = part.reshape(
                expert_count, capacity, half
            )


def run_expert(x, wg, wu, wd, expert_count, step_groups):
    groups, pipes, both, feat = x.shape
    rows = both // 2
    width, hidden = wg.shape
    half = feat // 2
    step_rows = step_groups * rows
    step_slots = step_rows // expert_count
    everything = groups * rows
    whole = lambda shape: pl.BlockSpec(shape, lambda s: (0, 0))
    flipped = pl.BlockSpec((hidden, step_rows), lambda s: (0, s))
    return pl.pallas_call(
        functools.partial(expert_kernel, expert_count),
        grid=(groups // step_groups,),
        in_specs=[
            pl.BlockSpec((step_groups, pipes, both, feat), lambda s: (s, 0, 0, 0)),
            whole((width, hidden)),
            whole((width, hidden)),
            whole((hidden, width)),
        ],
        out_specs=[
            flipped,
            flipped,
            flipped,
            pl.BlockSpec((pipes, step_rows, half), lambda s: (0, s, 0)),
            pl.BlockSpec((expert_count, pipes, step_slots, half), lambda s: (0, 0, s, 0)),
        ],
        out_shape=[jax.ShapeDtypeStruct((hidden, everything), BF16)] * 3
        + [
            jax.ShapeDtypeStruct((pipes, everything, half), BF16),
            jax.ShapeDtypeStruct((expert_count, pipes, everything // expert_count, half), BF16),
        ],
        compiler_params=pltpu.CompilerParams(vmem_limit_bytes=VMEM_LIMIT),
        name="expert",
        interpret=INTERPRET,
    )(x, wg, wu, wd)


def weight_kernel(x_ref, act_ref, gg_ref, ug_ref, dwg_ref, dwu_ref, dwd_ref):
    groups, _, both, feat = x_ref.shape
    rows = both // 2
    features = x_ref[:, 0, :rows, :].reshape(groups * rows, feat)
    cotangent = x_ref[:, 0, rows:, :].reshape(groups * rows, feat)
    dwg_ref[...] = dot(gg_ref[...], features).astype(BF16).T
    dwu_ref[...] = dot(ug_ref[...], features).astype(BF16).T
    dwd_ref[...] = dot(act_ref[...], cotangent).astype(BF16)


def run_weights(x, act, gg, ug):
    groups, pipes, both, feat = x.shape
    hidden, everything = act.shape
    whole = pl.BlockSpec((hidden, everything), lambda p: (0, 0))
    return pl.pallas_call(
        weight_kernel,
        grid=(pipes,),
        in_specs=[
            pl.BlockSpec((groups, 1, both, feat), lambda p: (0, p, 0, 0)),
            whole,
            whole,
            whole,
        ],
        out_specs=[
            pl.BlockSpec((feat, hidden), lambda p: (p, 0)),
            pl.BlockSpec((feat, hidden), lambda p: (p, 0)),
            pl.BlockSpec((hidden, feat), lambda p: (0, p)),
        ],
        out_shape=[
            jax.ShapeDtypeStruct((pipes * feat, hidden), BF16),
            jax.ShapeDtypeStruct((pipes * feat, hidden), BF16),
            jax.ShapeDtypeStruct((hidden, pipes * feat), BF16),
        ],
        compiler_params=pltpu.CompilerParams(vmem_limit_bytes=VMEM_LIMIT),
        name="weights",
        interpret=INTERPRET,
    )(x, act, gg, ug)


def combine_kernel(group_count, x_ref, slots_ref, out_ref):
    experts, _, slots, half = x_ref.shape
    capacity = slots // group_count
    tokens = slots_ref.shape[1]
    want = lax.broadcasted_iota(jnp.int32, (tokens, experts * capacity), 1)
    for d in range(group_count):
        rows = x_ref[:, 0, d * capacity : (d + 1) * capacity, :].reshape(experts * capacity, half)
        picked = (slots_ref[d, :, 0:1] == want) | (slots_ref[d, :, 1:2] == want)
        chosen = jnp.where(picked, 1.0, 0.0).astype(BF16)
        out_ref[0, d * tokens : (d + 1) * tokens, :] = dot(chosen, rows).astype(BF16)


def total_of(parts):
    total = parts[0].astype(F32)
    for k in range(1, parts.shape[0]):
        total = total + parts[k].astype(F32)
    return total.astype(BF16)


def run_combine(x, slots):
    experts, pipes, everything, half = x.shape
    group_count, tokens, _ = slots.shape
    return pl.pallas_call(
        functools.partial(combine_kernel, group_count),
        grid=(pipes,),
        in_specs=[
            pl.BlockSpec((experts, 1, everything, half), lambda p: (0, p, 0, 0)),
            pl.BlockSpec((group_count, tokens, 2), lambda p: (0, 0, 0)),
        ],
        out_specs=pl.BlockSpec((1, group_count * tokens, half), lambda p: (p, 0, 0)),
        out_shape=jax.ShapeDtypeStruct((pipes, group_count * tokens, half), BF16),
        compiler_params=pltpu.CompilerParams(vmem_limit_bytes=VMEM_LIMIT),
        name="combine",
        interpret=INTERPRET,
    )(x, slots)


def body(tokens, out_grad, gate_values, expert_ids, w_gate, w_up, w_down):
    expert_count = lax.axis_size("expert")
    group_count = lax.axis_size("dp")
    pipe_count = lax.axis_size("pipe")
    token_count, feat = tokens.shape
    capacity = max(token_count // 2, 2 * token_count // expert_count)
    slot_total = expert_count * capacity
    half = feat // 2
    slot_index = slot_indices(expert_ids, expert_count, capacity)
    picker, sent_rows, sent_grads = fill_slots(
        slot_index, gate_values, slot_total, tokens, out_grad
    )
    sent = jnp.concatenate(
        [
            sent_rows.reshape(expert_count, 1, capacity, feat),
            sent_grads.reshape(expert_count, 1, capacity, feat),
        ],
        axis=1,
    )
    received = lax.all_to_all(sent, "expert", split_axis=0, concat_axis=0, tiled=True)
    received = received.transpose(1, 0, 2, 3).reshape(1, 2 * slot_total, feat)
    gathered = lax.all_gather(received, ("dp", "pipe"), axis=0, tiled=True)
    column_slots = lax.all_gather(slot_index[None], "dp", axis=0, tiled=True)
    gathered, column_slots = lax.optimization_barrier((gathered, column_slots))
    x = gathered.reshape(group_count, pipe_count, 2 * slot_total, feat)
    act, gg, ug, ring, cross = run_expert(
        x, w_gate[0], w_up[0], w_down[0], expert_count, group_count // 4
    )
    over_pipe = lax.psum_scatter(ring, "pipe", scatter_dimension=0, tiled=True)
    crossed = lax.all_to_all(cross, "expert", split_axis=0, concat_axis=0, tiled=True)
    gate_weight_gradient, up_weight_gradient, grad_down = run_weights(x, act, gg, ug)
    summed = lax.psum_scatter(
        over_pipe.reshape(group_count, slot_total, half), "dp", scatter_dimension=0, tiled=True
    )
    column = run_combine(crossed, column_slots)
    column = lax.all_to_all(column, "pipe", split_axis=0, concat_axis=0, tiled=True)
    column = total_of(column)
    column = lax.all_to_all(
        column.reshape(group_count, token_count, half), "dp", split_axis=0, concat_axis=0, tiled=True
    )
    right = total_of(column)
    returned = lax.all_to_all(
        summed.reshape(expert_count, capacity, half), "expert", split_axis=0, concat_axis=0, tiled=True
    )
    left = jnp.einsum(
        "st,sq->tq", picker, returned.reshape(slot_total, half), preferred_element_type=F32
    ).astype(BF16)
    grad_tokens = jnp.concatenate([left, right], axis=1)
    return (
        grad_tokens,
        gate_weight_gradient[None],
        up_weight_gradient[None],
        grad_down[None],
    )


def solution(mesh):
    rows = P(("expert", "dp"), "pipe")
    pairs = P(("expert", "dp"), None)
    wide = P("expert", None, ("dp", "pipe"))
    tall = P("expert", ("dp", "pipe"), None)
    return jax.shard_map(
        body,
        mesh=mesh,
        in_specs=(rows, rows, pairs, pairs, wide, wide, tall),
        out_specs=(rows, wide, wide, tall),
        check_vma=False,
    )
```

time: 473 us -> 260 us (0.55)
  waiting for transfers between devices: 359 us -> 146 us
  matrix products: 42.8 us -> 1.56 us
  Pallas kernels: 0 us -> 31.2 us
  blocking collectives: 22 us -> 43.9 us
  local copies, waits for them, and re-layouts: 21.8 us -> 4.28 us
  starting transfers between devices: 9.19 us -> 15.8 us
    reduce_scatter x1 -> x2, waiting for transfers between devices: 206 us -> 33.1 us  [the longest x1 33.1 us: body(): over_pipe = lax.psum_scatter(ring, 'pipe', scatter_dimension=0, tiled=True)]
    all_gather x2 -> x1, waiting for transfers between devices: 152 us -> 104 us  [body(): gathered = lax.all_gather(received, ('dp', 'pipe'), axis=0, tiled=True)]
    dot_general x11 -> x3, matrix products: 42.8 us -> 1.56 us  [the longest x1 1.06 us: fill_slots(): jnp.dot(picker, features, preferred_element_type=F32).astype(BF16)]
    pallas_call x0 -> x3, Pallas kernels: none -> 31.2 us  [the longest x1 17 us: run_expert(): pl.pallas_call(functools.partial(expert_kernel, expert_count), grid=(grou...]
    dot_general x2 -> x0, local copies, waits for them, and re-layouts: 17.3 us -> none  [the longest x1 8.77 us: body(): jnp.einsum('cjb,cvji->bvi', swiglu_activation, gathered_gradients, prefer...]
    all_gather x0 -> x1, blocking collectives: none -> 15.4 us  [body(): column_slots = lax.all_gather(slot_index[None], 'dp', axis=0, tiled=True)]
    all_to_all x1 -> x3, waiting for transfers between devices: 0.01 us -> 8.51 us  [the longest x1 4.95 us: body(): lax.all_to_all(summed.reshape(expert_count, capacity, half), 'expert', sp...]
    all_to_all x1 -> x3, starting transfers between devices: 9.06 us -> 15.8 us  [the longest x1 6.02 us: body(): lax.all_to_all(summed.reshape(expert_count, capacity, half), 'expert', sp...]
  transfers between devices with their start and end apart: 4 -> 6, of which waited for: 3 -> 4; matrix products, arithmetic and copies ran while one was open for 10% -> 1% of each run, Pallas kernels for 0% -> 5%
where the time goes in v1:
time: 260 us
  waiting for transfers between devices  146 us (56%)
  blocking collectives  43.9 us (17%)
  Pallas kernels  31.2 us (12%)
  starting transfers between devices  15.8 us (6%)
  between operations  13.8 us (5%)
  local copies, waits for them, and re-layouts  4.28 us (2%)
  other arithmetic  3.36 us (1%)
    all_gather x1, waiting for transfers between devices, body(): gathered = lax.all_gather(received, ('dp', 'pipe'), axis=0, tiled=True)  104 us
    reduce_scatter x1, waiting for transfers between devices, body(): over_pipe = lax.psum_scatter(ring, 'pipe', scatter_dimension=0, tiled=True)  33.1 us
    pallas_call x1, Pallas kernels, run_expert(): pl.pallas_call(functools.partial(expert_kernel, expert_count), grid=(grou...  17 us
    all_gather x1, blocking collectives, body(): column_slots = lax.all_gather(slot_index[None], 'dp', axis=0, tiled=True)  15.4 us
    all_to_all x1, blocking collectives, body(): lax.all_to_all(column, 'pipe', split_axis=0, concat_axis=0, tiled=True)  14.9 us
    all_to_all x1, blocking collectives, body(): lax.all_to_all(sent, 'expert', split_axis=0, concat_axis=0, tiled=True)  13.6 us
    pallas_call x1, Pallas kernels, run_weights(): pl.pallas_call(weight_kernel, grid=(pipes,), in_specs=[pl.BlockSpec((grou...  9.9 us
    all_to_all x1, starting transfers between devices, body(): lax.all_to_all(summed.reshape(expert_count, capacity, half), 'expert', sp...  6.02 us
  transfers between devices with their start and end apart: 6, of which 4 were waited for; matrix products, arithmetic and copies ran while one was open for 1% of the time, Pallas kernels for 5%

profile of v1, /device:TPU:1, one launch (start us, length us, event | category | flops | bytes accessed | tf_op | source)
XLA Modules:
  0.0 259.8 jit_solution(15074868014272729564)
XLA Ops:
  7.2 0.8 copy.49
  8.0 0.1 eq.29
  8.1 0.1 fusion
  8.2 0.1 reduce_window_sum.11
  8.3 0.2 select_reduce_fusion.1
  8.5 0.1 reduce_sum.21
  8.6 0.1 copy.50
  8.6 0.7 multiply_add_fusion
  9.3 0.1 fusion.1
  9.4 0.8 select_reduce_fusion
  10.2 0.4 convolution_convert_fusion
  10.6 1.1 convolution_convert_fusion.1
  11.7 13.6 %all_to_all.25 = bf16[8,2,16,768]{3,2,1,0:T(8,128)(2,1)S(1)} all-to-all(bf16[8,2,16,768]{3,2,1,0:T(8,128)(2,1)S(1)} %pad_maximum_fusion), channel_id=1, replica_groups=mesh['expert'=8,'dp'=8,'pipe'=4] {'expert'}, dimensions={0} | all-to-all | bytes 786432 | tf_op jit(solution)/shard_map/all_to_all | solution.py:210
  25.3 0.8 copy.53
  26.1 0.0 reduce-scatter.3.cloned.1.call-start
  26.2 15.4 %all-gather.1 = s32[8,32,2]{1,2,0:T(2,128)S(1)} all-gather(s32[1,32,2]{1,2,0:T(2,128)S(1)} %bitcast.40), channel_id=2, replica_groups=mesh['expert'=8,'dp'=8,'pipe'=4] {'dp'}, dimensions={0}, use_global_device_ids=true | all-gather | bytes 2304 | tf_op jit(solution)/shard_map/all_gather | solution.py:213
  41.6 104.2 %all-gather.4.cloned.1.call-done = bf16[32,256,768]{2,1,0:T(8,128)(2,1)} async-done(((bf16[1,256,768]{2,1,0:T(8,128)(2,1)}), bf16[32,256,768]{2,1,0:T(8,128)(2,1)}) %all-gather.4.cloned.1.call-update) | async-done | bytes 12582928 | tf_op jit(solution)/shard_map/all_gather | solution.py:212
  145.7 17.0 %expert.1 = (bf16[256,1024]{1,0:T(8,128)(2,1)}, bf16[256,1024]{1,0:T(8,128)(2,1)}, bf16[256,1024]{1,0:T(8,128)(2,1)}, bf16[4,1024,384]{2,1,0:T(8,128)(2,1)}, bf16[8,4,128,384]{3,2,1,0:T(8,128)(2,1)}) custom-call(bf16[8,4,256,768]{3,2,1,0:T(8,128)(2,1)} %bitcast.29, bf16[3072,256]{1,0:T(8,128)(2,1)} %bitcast.31, bf16[3072,256]{1,0:T(8,128)(2,1)} %bitcast.32, ...), custom_call_target="tpu_custom_call" | custom-call | tf_op jit(solution)/shard_map/expert/pallas_call | solution.py:88
  162.7 5.7 %all-to-all-start.2 = ((bf16[8,4,128,384]{3,2,1,0:T(8,128)(2,1)}), bf16[8,4,128,384]{3,2,1,0:T(8,128)(2,1)S(1)}, u32[]{:S(2)}, u32[]{:S(2)}) async-start(bf16[8,4,128,384]{3,2,1,0:T(8,128)(2,1)} %get-tuple-element.16), calls=%async_computation.4 | async-start | bytes 6291456 | tf_op jit(solution)/shard_map/all_to_all | solution.py:220
  168.4 33.1 %reduce-scatter.3.cloned.1.call-done = bf16[1,1024,384]{2,1,0:T(8,128)(2,1)} async-done(((bf16[4,1024,384]{2,1,0:T(8,128)(2,1)}), bf16[1,1024,384]{2,1,0:T(8,128)(2,1)}) %reduce-scatter.3.cloned.1.call-update) | async-done | bytes 786448 | tf_op jit(solution)/shard_map/reduce_scatter | solution.py:219
  201.5 0.8 copy.54.slots_ref
  202.3 3.6 %all-to-all-done.2.x_ref = bf16[8,4,128,384]{3,2,1,0:T(8,128)(2,1)S(1)} async-done(((bf16[8,4,128,384]{3,2,1,0:T(8,128)(2,1)}), bf16[8,4,128,384]{3,2,1,0:T(8,128)(2,1)S(1)}, u32[]{:S(2)}, u32[]{:S(2)}) %all-to-all-start.2) | async-done | bytes 3145760 | tf_op jit(solution)/shard_map/all_to_all | solution.py:220
  205.8 1.7 copy-done.1
  207.5 4.3 %combine.1 = bf16[4,256,384]{2,1,0:T(8,128)(2,1)} custom-call(bf16[8,4,128,384]{3,2,1,0:T(8,128)(2,1)} %copy-done.1, s32[8,32,2]{2,1,0:T(8,128)} %copy.54.slots_ref), custom_call_target="tpu_custom_call" | custom-call | tf_op jit(solution)/shard_map/combine/pallas_call | solution.py:176
  211.8 14.9 %all_to_all.26 = bf16[4,256,384]{2,1,0:T(8,128)(2,1)S(1)} all-to-all(bf16[4,256,384]{2,1,0:T(8,128)(2,1)} %combine.1), channel_id=1, replica_groups=mesh['expert'=8,'dp'=8,'pipe'=4] {'pipe'}, dimensions={0} | all-to-all | bytes 1572864 | tf_op jit(solution)/shard_map/all_to_all | solution.py:226
  226.7 0.8 add_convert_fusion
  227.5 4.1 %all-to-all-start.4 = ((bf16[8,32,384]{2,1,0:T(8,128)(2,1)}), bf16[8,32,384]{2,1,0:T(8,128)(2,1)S(1)}, u32[]{:S(2)}, u32[]{:S(2)}) async-start(bf16[8,32,384]{2,1,0:T(8,128)(2,1)} %bitcast.14), calls=%async_computation.6 | async-start | bytes 393216 | tf_op jit(solution)/shard_map/all_to_all | solution.py:228
  231.5 9.9 %weights.1 = (bf16[3072,256]{1,0:T(8,128)(2,1)}, bf16[3072,256]{1,0:T(8,128)(2,1)}, bf16[256,3072]{1,0:T(8,128)(2,1)}) custom-call(bf16[8,4,256,768]{3,2,1,0:T(8,128)(2,1)} %bitcast.30, bf16[256,1024]{1,0:T(8,128)(2,1)} %get-tuple-element.18.act_ref, bf16[256,1024]{1,0:T(8,128)(2,1)} %get-tuple-element.19.gg_ref, bf16[256,1024]{1,0:T(8,128)(2,1)} %get-tuple-element.20.ug_ref), custom_call_target="tpu_custom_call" | custom-call | tf_op jit(solution)/shard_map/weights/pallas_call | solution.py:129
  241.5 6.0 %all-to-all-start.1 = ((bf16[8,16,384]{2,1,0:T(8,128)(2,1)}), bf16[8,16,384]{2,1,0:T(8,128)(2,1)S(1)}, u32[]{:S(2)}, u32[]{:S(2)}) async-start(bf16[8,16,384]{2,1,0:T(8,128)(2,1)} %bitcast.39), calls=%async_computation.3 | async-start | bytes 196608 | tf_op jit(solution)/shard_map/all_to_all | solution.py:232
  247.5 4.9 %all-to-all-done.1 = bf16[8,16,384]{2,1,0:T(8,128)(2,1)S(1)} async-done(((bf16[8,16,384]{2,1,0:T(8,128)(2,1)}), bf16[8,16,384]{2,1,0:T(8,128)(2,1)S(1)}, u32[]{:S(2)}, u32[]{:S(2)}) %all-to-all-start.1) | async-done | bytes 98336 | tf_op jit(solution)/shard_map/all_to_all | solution.py:232
  252.5 0.1 convolution_convert_fusion.2
  252.6 0.6 pad_maximum_fusion.1
  (12 shorter events, 0.2 us)
Async XLA Ops:
  7.2 3.0 %copy-start = (bf16[32,768]{1,0:T(8,128)(2,1)S(1)}, bf16[32,768]{1,0:T(8,128)(2,1)}, u32[]{:S(2)}) copy-start(bf16[32,768]{1,0:T(8,128)(2,1)} %param.8) | copy-start | bytes 147460
  7.2 138.5 %all-gather.4.cloned.1.call-start = ((), (), s32[]{:S(2)}) async-start(), calls=%async_computation.7 | async-start | bytes 12976128 | tf_op jit(solution)/shard_map/all_gather | solution.py:212
  26.1 175.4 %reduce-scatter.3.cloned.1.call-start = ((), (), s32[]{:S(2)}) async-start(), calls=%async_computation.8 | async-start | bytes 3932160 | tf_op jit(solution)/shard_map/reduce_scatter | solution.py:219
  162.7 43.1 %all-to-all-start.2 = ((bf16[8,4,128,384]{3,2,1,0:T(8,128)(2,1)}), bf16[8,4,128,384]{3,2,1,0:T(8,128)(2,1)S(1)}, u32[]{:S(2)}, u32[]{:S(2)}) async-start(bf16[8,4,128,384]{3,2,1,0:T(8,128)(2,1)} %get-tuple-element.16), calls=%async_computation.4 | async-start | bytes 6291456 | tf_op jit(solution)/shard_map/all_to_all | solution.py:220
  168.4 73.1 %reduce-scatter.5.cloned.1.call-start = ((), (), s32[]{:S(2)}) async-start(), calls=%async_computation.9 | async-start | bytes 884736 | tf_op jit(solution)/shard_map/reduce_scatter | solution.py:222
  205.8 1.7 copy-start.1
  227.5 14.0 %all-to-all-start.4 = ((bf16[8,32,384]{2,1,0:T(8,128)(2,1)}), bf16[8,32,384]{2,1,0:T(8,128)(2,1)S(1)}, u32[]{:S(2)}, u32[]{:S(2)}) async-start(bf16[8,32,384]{2,1,0:T(8,128)(2,1)} %bitcast.14), calls=%async_computation.6 | async-start | bytes 393216 | tf_op jit(solution)/shard_map/all_to_all | solution.py:228
  241.5 11.0 %all-to-all-start.1 = ((bf16[8,16,384]{2,1,0:T(8,128)(2,1)}), bf16[8,16,384]{2,1,0:T(8,128)(2,1)S(1)}, u32[]{:S(2)}, u32[]{:S(2)}) async-start(bf16[8,16,384]{2,1,0:T(8,128)(2,1)} %bitcast.39), calls=%async_computation.3 | async-start | bytes 196608 | tf_op jit(solution)/shard_map/all_to_all | solution.py:232
Sparse Core Ops, SparseCore 0:
  26.2 119.4 all-gather.3
  162.8 38.5 reduce-scatter.2
  204.0 34.4 reduce-scatter.4

commit v2 on v1

v2 whole, which is shorter than its diff:
```python
import functools

import jax
import jax.numpy as jnp
from jax import lax
from jax.experimental import pallas as pl
from jax.experimental.pallas import tpu as pltpu
from jax.sharding import PartitionSpec as P


F32 = jnp.float32
BF16 = jnp.bfloat16
INTERPRET = False
VMEM_LIMIT = 58 * 1024 * 1024
NN = (((1,), (0,)), ((), ()))
NT = (((1,), (1,)), ((), ()))


def dot(a, b, dims=NN):
    return lax.dot_general(a, b, dims, preferred_element_type=F32)


def slot_indices(expert_ids, expert_count, capacity):
    choices_flat = expert_ids.reshape(-1)
    one_hot = (choices_flat[:, None] == jnp.arange(expert_count, dtype=jnp.int32)[None, :]).astype(
        jnp.int32
    )
    ranks = jnp.cumsum(one_hot, axis=0) - 1
    return (choices_flat * capacity + jnp.sum(one_hot * ranks, axis=1)).reshape(-1, 2)


def fill_slots(slot_index, gate_values, slot_total, features, cotangent):
    hits = jnp.arange(slot_total, dtype=jnp.int32)[:, None, None] == slot_index[None, :, :]
    picker = jnp.any(hits, axis=2).astype(BF16)
    weighting = jnp.sum(jnp.where(hits, gate_values[None, :, :], 0.0), axis=2)
    sent_rows = jnp.dot(picker, features, preferred_element_type=F32).astype(BF16)
    sent_grads = jnp.dot(weighting, cotangent.astype(F32), precision=lax.Precision.HIGHEST).astype(
        BF16
    )
    return (picker, sent_rows, sent_grads)


def expert_kernel(expert_count, order_ref, a_ref, b0_ref, b1_ref, b3_ref, b2x_ref, b2y_ref, wg_ref, wu_ref, wd_ref, act_ref, gg_ref, ug_ref, ring_ref, cross_ref):
    groups, pipes, both, half = a_ref.shape
    rows = both // 2
    total = groups * rows
    feat = 2 * half
    capacity = rows // expert_count
    early = pl.program_id(0) < pl.num_programs(0) // 2
    pieces = []
    for p in range(pipes):
        pieces.append((a_ref[:, p], p * feat))
    opposite = jnp.where(early, b2x_ref[...], b2y_ref[...])
    for k, value in enumerate((b0_ref[...], b3_ref[...], opposite, b1_ref[...])):
        pieces.append((value, pl.multiple_of(order_ref[k] * feat + half, 128)))
    gate = up = act_grad = None
    for value, start in pieces:
        features = value[:, :rows, :].reshape(total, half)
        cotangent = value[:, rows:, :].reshape(total, half)
        cols = pl.ds(start, half)
        g = dot(features, wg_ref[cols, :])
        u = dot(features, wu_ref[cols, :])
        a = dot(cotangent, wd_ref[:, cols], NT)
        gate = g if gate is None else gate + g
        up = u if up is None else up + u
        act_grad = a if act_grad is None else act_grad + a
    sig = jax.nn.sigmoid(gate)
    linear = gate * sig
    act = (linear * up).astype(BF16)
    gate_grad = (act_grad * up * (sig * (1.0 + gate * (1.0 - sig)))).astype(BF16)
    up_grad = (act_grad * linear).astype(BF16)
    act_ref[...] = act.T
    gg_ref[...] = gate_grad.T
    ug_ref[...] = up_grad.T
    for p in range(pipes):
        cols = slice(p * feat, (p + 1) * feat)
        back = (dot(gate_grad, wg_ref[cols, :], NT) + dot(up_grad, wu_ref[cols, :], NT)).astype(BF16)
        for d in range(groups):
            part = back[d * rows : (d + 1) * rows].reshape(expert_count, capacity, feat)
            ring_ref[p, :, d * capacity : (d + 1) * capacity, :] = part[:, :, :half]
            cross_ref[:, p, d * capacity : (d + 1) * capacity, :] = part[:, :, half:]


def run_expert(order, a, b, wg, wu, wd, expert_count, step_groups):
    groups, pipes, both, half = a.shape
    rows = both // 2
    width, hidden = wg.shape
    step_rows = step_groups * rows
    step_slots = step_rows // expert_count
    everything = groups * rows
    steps = groups // step_groups
    whole = lambda shape: pl.BlockSpec(shape, lambda s, o: (0, 0))
    flipped = pl.BlockSpec((hidden, step_rows), lambda s, o: (0, s))
    piece = pl.BlockSpec((step_groups, both, half), lambda s, o: (s, 0, 0))
    return pl.pallas_call(
        functools.partial(expert_kernel, expert_count),
        grid_spec=pltpu.PrefetchScalarGridSpec(
            num_scalar_prefetch=1,
            grid=(steps,),
            in_specs=[
                pl.BlockSpec((step_groups, pipes, both, half), lambda s, o: (s, 0, 0, 0)),
                piece,
                piece,
                piece,
                pl.BlockSpec(
                    (step_groups, both, half), lambda s, o: (jnp.minimum(s, steps // 2 - 1), 0, 0)
                ),
                pl.BlockSpec(
                    (step_groups, both, half), lambda s, o: (jnp.maximum(s - steps // 2, 0), 0, 0)
                ),
                whole((width, hidden)),
                whole((width, hidden)),
                whole((hidden, width)),
            ],
            out_specs=[
                flipped,
                flipped,
                flipped,
                pl.BlockSpec((pipes, expert_count, step_slots, half), lambda s, o: (0, 0, s, 0)),
                pl.BlockSpec((expert_count, pipes, step_slots, half), lambda s, o: (0, 0, s, 0)),
            ],
        ),
        out_shape=[jax.ShapeDtypeStruct((hidden, everything), BF16)] * 3
        + [
            jax.ShapeDtypeStruct((pipes, expert_count, everything // expert_count, half), BF16),
            jax.ShapeDtypeStruct((expert_count, pipes, everything // expert_count, half), BF16),
        ],
        compiler_params=pltpu.CompilerParams(vmem_limit_bytes=VMEM_LIMIT),
        name="expert",
        interpret=INTERPRET,
    )(order, a, *b, wg, wu, wd)


def weight_kernel(order_ref, a_ref, b0_ref, b1_ref, b3_ref, b2x_ref, b2y_ref, act_ref, gg_ref, ug_ref, dwg_ref, dwu_ref, dwd_ref):
    groups, _, both, half = a_ref.shape
    rows = both // 2
    step = pl.program_id(0)
    count = pl.num_programs(0) // 2

    def work(value):
        features = value[:, :rows, :].reshape(groups * rows, half)
        cotangent = value[:, rows:, :].reshape(groups * rows, half)
        dwg_ref[...] = dot(gg_ref[...], features).astype(BF16).T
        dwu_ref[...] = dot(ug_ref[...], features).astype(BF16).T
        dwd_ref[...] = dot(act_ref[...], cotangent).astype(BF16)

    pl.when(step < count)(lambda: work(a_ref[:, 0]))
    pl.when(step == count)(lambda: work(b0_ref[...]))
    pl.when(step == count + 1)(lambda: work(b3_ref[...]))
    pl.when(step == count + 2)(
        lambda: work(jnp.concatenate([b2x_ref[...], b2y_ref[...]], axis=0))
    )
    pl.when(step == count + 3)(lambda: work(b1_ref[...]))


def run_weights(order, a, b, act, gg, ug):
    groups, pipes, both, half = a.shape
    hidden, everything = act.shape
    whole = pl.BlockSpec((hidden, everything), lambda s, o: (0, 0))
    piece = lambda v: pl.BlockSpec(v.shape, lambda s, o: (0, 0, 0))

    def place(s, o):
        return jnp.where(s < pipes, 2 * s, 2 * o[jnp.maximum(s - pipes, 0)] + 1)

    return pl.pallas_call(
        weight_kernel,
        grid_spec=pltpu.PrefetchScalarGridSpec(
            num_scalar_prefetch=1,
            grid=(2 * pipes,),
            in_specs=[
                pl.BlockSpec(
                    (groups, 1, both, half), lambda s, o: (0, jnp.minimum(s, pipes - 1), 0, 0)
                ),
            ]
            + [piece(v) for v in b]
            + [whole] * 3,
            out_specs=[
                pl.BlockSpec((half, hidden), lambda s, o: (place(s, o), 0)),
                pl.BlockSpec((half, hidden), lambda s, o: (place(s, o), 0)),
                pl.BlockSpec((hidden, half), lambda s, o: (0, place(s, o))),
            ],
        ),
        out_shape=[
            jax.ShapeDtypeStruct((2 * pipes * half, hidden), BF16),
            jax.ShapeDtypeStruct((2 * pipes * half, hidden), BF16),
            jax.ShapeDtypeStruct((hidden, 2 * pipes * half), BF16),
        ],
        compiler_params=pltpu.CompilerParams(vmem_limit_bytes=VMEM_LIMIT),
        name="weights",
        interpret=INTERPRET,
    )(order, a, *b, act, gg, ug)


def combine_kernel(x_ref, slots_ref, out_ref):
    experts, _, slots, half = x_ref.shape
    group_count = slots_ref.shape[0]
    capacity = slots // group_count
    tokens = out_ref.shape[1] // group_count
    want = lax.broadcasted_iota(jnp.int32, (experts * capacity, tokens), 0).astype(F32)
    for d in range(group_count):
        rows = x_ref[:, 0, d * capacity : (d + 1) * capacity, :].reshape(experts * capacity, half)
        ids = slots_ref[d].astype(F32)
        picked = (ids[0:1, :tokens] == want) | (ids[1:2, :tokens] == want)
        chosen = jnp.where(picked, 1.0, 0.0).astype(BF16)
        out_ref[0, d * tokens : (d + 1) * tokens, :] = dot(
            chosen, rows, (((0,), (0,)), ((), ()))
        ).astype(BF16)


def run_combine(x, slots, tokens):
    experts, pipes, everything, half = x.shape
    group_count = slots.shape[0]
    return pl.pallas_call(
        combine_kernel,
        grid=(pipes,),
        in_specs=[
            pl.BlockSpec((experts, 1, everything, half), lambda p: (0, p, 0, 0)),
            pl.BlockSpec(slots.shape, lambda p: (0, 0, 0)),
        ],
        out_specs=pl.BlockSpec((1, group_count * tokens, half), lambda p: (p, 0, 0)),
        out_shape=jax.ShapeDtypeStruct((pipes, group_count * tokens, half), BF16),
        compiler_params=pltpu.CompilerParams(vmem_limit_bytes=VMEM_LIMIT),
        name="combine",
        interpret=INTERPRET,
    )(x, slots)


def total_of(parts):
    total = parts[0].astype(F32)
    for k in range(1, parts.shape[0]):
        total = total + parts[k].astype(F32)
    return total.astype(BF16)


def shift(x, axis, by):
    count = lax.axis_size(axis)
    return lax.ppermute(x, axis, [(k, (k + by) % count) for k in range(count)])


def place_kernel(moves, at_ref, *refs):
    count = 1 + max(m[0] for m in moves)
    sems = refs[-1]
    copies = []
    for n, (source, begin, size, columns, target, place, row) in enumerate(moves):
        copies.append(
            pltpu.make_async_copy(
                refs[source].at[begin : begin + size, :columns],
                refs[count + target].at[at_ref[place], row : row + size, :],
                sems.at[n],
            )
        )
    for copy in copies:
        copy.start()
    for copy in copies:
        copy.wait()


def run_place(at, pieces, moves, shapes):
    return pl.pallas_call(
        functools.partial(place_kernel, moves),
        in_specs=[pl.BlockSpec(memory_space=pltpu.SMEM)]
        + [pl.BlockSpec(memory_space=pl.ANY)] * len(pieces),
        out_specs=[pl.BlockSpec(memory_space=pl.ANY)] * len(shapes),
        out_shape=[jax.ShapeDtypeStruct(shape, BF16) for shape in shapes],
        scratch_shapes=[pltpu.SemaphoreType.DMA((len(moves),))],
        compiler_params=pltpu.CompilerParams(vmem_limit_bytes=VMEM_LIMIT),
        name="place",
        interpret=INTERPRET,
    )(at, *pieces)


def groups_ring(x, rows):
    whole, width = x.shape
    cut = (whole // 2 + 15) // 16 * 16
    up1, down1 = shift(x, "dp", 1), shift(x, "dp", -1)
    up2, down2 = shift(up1, "dp", 1), shift(down1, "dp", -1)
    up3, down3 = shift(up2, "dp", 1), shift(down2, "dp", -1)
    far_up, far_down = shift(up3[:cut], "dp", 1), shift(down3[cut:], "dp", -1)
    count = lax.axis_size("dp")
    at = (lax.axis_index("dp") + jnp.arange(count, dtype=jnp.int32)) % count
    pieces = (x, down1, down2, down3, up3, up2, up1, far_up, far_down)
    moves = []
    for n, place in enumerate((0, 1, 2, 3, 5, 6, 7)):
        moves.append((n, 0, rows, width, 0, place, 0))
        moves.append((n, rows, whole - rows, 128, 1, place, 0))
    moves.append((7, 0, cut, width, 0, 4, 0))
    moves.append((8, 0, rows - cut, width, 0, 4, cut))
    moves.append((8, rows - cut, whole - rows, 128, 1, 4, 0))
    return run_place(at, pieces, tuple(moves), [(count, rows, width), (count, whole - rows, 128)])


def pipes_direct(x):
    pieces = (x, shift(x, "pipe", -1), shift(x, "pipe", 2), shift(x, "pipe", 1))
    count = lax.axis_size("pipe")
    at = (lax.axis_index("pipe") + jnp.arange(count, dtype=jnp.int32)) % count
    rows, width = x.shape
    moves = tuple((n, 0, rows, width, 0, n, 0) for n in range(count))
    return run_place(at, pieces, moves, [(count, rows, width)])[0]


def pipes_ring(x):
    cut = x.shape[0] // 2
    up1, down1 = shift(x, "pipe", 1), shift(x, "pipe", -1)
    return x, up1, down1, shift(up1[:cut], "pipe", 1), shift(down1[cut:], "pipe", -1)


def body(tokens, out_grad, gate_values, expert_ids, w_gate, w_up, w_down):
    expert_count = lax.axis_size("expert")
    group_count = lax.axis_size("dp")
    pipe_count = lax.axis_size("pipe")
    token_count, feat = tokens.shape
    capacity = max(token_count // 2, 2 * token_count // expert_count)
    slot_total = expert_count * capacity
    half = feat // 2
    slot_index = slot_indices(expert_ids, expert_count, capacity)
    _, sent_rows, sent_grads = fill_slots(slot_index, gate_values, slot_total, tokens, out_grad)
    sent = jnp.concatenate(
        [
            sent_rows.reshape(expert_count, 1, capacity, feat),
            sent_grads.reshape(expert_count, 1, capacity, feat),
        ],
        axis=1,
    )
    received = lax.all_to_all(sent, "expert", split_axis=0, concat_axis=0, tiled=True)
    received = received.transpose(1, 0, 2, 3).reshape(2 * slot_total, feat)
    slots = jnp.pad(slot_index.T.astype(BF16), ((0, 14), (0, half - token_count)))
    ringed, column_slots = groups_ring(
        jnp.concatenate([received[:, half:], slots], axis=0), 2 * slot_total
    )
    b = pipes_ring(ringed)
    a = lax.all_gather(pipes_direct(received[:, :half])[None], "dp", axis=0, tiled=True)
    me = lax.axis_index("pipe")
    order = (me + jnp.arange(pipe_count, dtype=jnp.int32)) % pipe_count
    act, gg, ug, ring, cross = run_expert(
        order, a, b, w_gate[0], w_up[0], w_down[0], expert_count, group_count // 4
    )
    over_pipe = lax.psum_scatter(
        ring.reshape(pipe_count, -1, half), "pipe", scatter_dimension=0, tiled=True
    )
    crossed = lax.all_to_all(cross, "expert", split_axis=0, concat_axis=0, tiled=True)
    gate_weight_gradient, up_weight_gradient, grad_down = run_weights(order, a, b, act, gg, ug)
    crossed, gate_weight_gradient = lax.optimization_barrier((crossed, gate_weight_gradient))
    right = run_combine(crossed, column_slots, token_count)
    right = lax.all_to_all(right, "pipe", split_axis=0, concat_axis=0, tiled=True)
    right = total_of(right)
    left = lax.all_to_all(
        over_pipe.reshape(expert_count, 1, -1, half), "expert", split_axis=0, concat_axis=0, tiled=True
    )
    left = run_combine(left, column_slots, token_count)[0]
    column = jnp.concatenate([left, right], axis=1).reshape(group_count, token_count, feat)
    column = lax.all_to_all(column, "dp", split_axis=0, concat_axis=0, tiled=True)
    return (
        total_of(column),
        gate_weight_gradient[None],
        up_weight_gradient[None],
        grad_down[None],
    )


def solution(mesh):
    rows = P(("expert", "dp"), "pipe")
    pairs = P(("expert", "dp"), None)
    wide = P("expert", None, ("dp", "pipe"))
    tall = P("expert", ("dp", "pipe"), None)

    return jax.shard_map(
        body,
        mesh=mesh,
        in_specs=(rows, rows, pairs, pairs, wide, wide, tall),
        out_specs=(rows, wide, wide, tall),
        check_vma=False,
    )
```

time: 260 us -> 349 us (1.34)
  Pallas kernels: 31.2 us -> 117 us
  waiting for transfers between devices: 146 us -> 120 us
  starting transfers between devices: 15.8 us -> 37 us
  blocking collectives: 43.9 us -> 47.5 us
    all_gather x1, waiting for transfers between devices: 104 us -> 0.01 us  [body(): lax.all_gather(pipes_direct(received[:, :half])[None], 'dp', axis=0, tile...]
    pallas_call x3 -> x6, Pallas kernels: 31.2 us -> 117 us  [the longest x2 76.2 us: run_place(): pl.pallas_call(functools.partial(place_kernel, moves), in_specs=[pl.Block...]
    ppermute x0 -> x15, waiting for transfers between devices: none -> 84.5 us  [shift(): return lax.ppermute(x, axis, [(k, (k + by) % count) for k in range(count)])]
    reduce_scatter x2 -> x1, waiting for transfers between devices: 33.1 us -> 0.01 us  [body(): lax.psum_scatter(ring.reshape(pipe_count, -1, half), 'pipe', scatter_dime...]
    ppermute x0 -> x15, starting transfers between devices: none -> 22.8 us  [shift(): return lax.ppermute(x, axis, [(k, (k + by) % count) for k in range(count)])]
    all_to_all x1, waiting for transfers between devices: 3.55 us -> 23 us  [body(): lax.all_to_all(cross, 'expert', split_axis=0, concat_axis=0, tiled=True)]
    all_to_all x1 -> x2, blocking collectives: 14.9 us -> 33.8 us  [the longest x1 18.6 us: body(): lax.all_to_all(column, 'dp', split_axis=0, concat_axis=0, tiled=True)]
    all_gather x1 -> x0, blocking collectives: 15.4 us -> none  [body(): column_slots = lax.all_gather(slot_index[None], 'dp', axis=0, tiled=True)]
  transfers between devices with their start and end apart: 6 -> 19, of which waited for: 4 -> 12; matrix products, arithmetic and copies ran while one was open for 1% -> 0% of each run, Pallas kernels for 5% -> 20%
where the time goes in v2:
time: 349 us; the launch traced here: 348 us
  waiting for transfers between devices  120 us (34%)
  Pallas kernels  117 us (34%)
  blocking collectives  47.5 us (14%)
  starting transfers between devices  37 us (11%)
  between operations  14.4 us (4%)
  local copies, waits for them, and re-layouts  5.91 us (2%)
  other arithmetic  4.77 us (1%)
    ppermute x15, waiting for transfers between devices, shift(): return lax.ppermute(x, axis, [(k, (k + by) % count) for k in range(count)])  84.5 us
    pallas_call x2, Pallas kernels, run_place(): pl.pallas_call(functools.partial(place_kernel, moves), in_specs=[pl.Block...  76.2 us
    all_to_all x1, waiting for transfers between devices, body(): lax.all_to_all(cross, 'expert', split_axis=0, concat_axis=0, tiled=True)  23 us
    ppermute x15, starting transfers between devices, shift(): return lax.ppermute(x, axis, [(k, (k + by) % count) for k in range(count)])  22.8 us
    pallas_call x1, Pallas kernels, run_expert(): pl.pallas_call(functools.partial(expert_kernel, expert_count), grid_spec=...  20.2 us
    all_to_all x1, blocking collectives, body(): lax.all_to_all(column, 'dp', split_axis=0, concat_axis=0, tiled=True)  18.6 us
    all_to_all x1, blocking collectives, body(): lax.all_to_all(right, 'pipe', split_axis=0, concat_axis=0, tiled=True)  15.2 us
    pallas_call x1, Pallas kernels, run_weights(): pl.pallas_call(weight_kernel, grid_spec=pltpu.PrefetchScalarGridSpec(num_...  14.4 us
  transfers between devices with their start and end apart: 19, of which 12 were waited for; matrix products, arithmetic and copies ran while one was open for 0% of the time, Pallas kernels for 20%

profile of v2, /device:TPU:1, one launch (start us, length us, event | category | flops | bytes accessed | tf_op | source)
XLA Modules:
  0.0 347.8 jit_solution(17144824541352456112)
XLA Ops:
  11.7 13.6 %all_to_all.25 = bf16[8,2,16,768]{3,2,1,0:T(8,128)(2,1)S(1)} all-to-all(bf16[8,2,16,768]{3,2,1,0:T(8,128)(2,1)S(1)} %pad_maximum_fusion), channel_id=1, replica_groups=mesh['expert'=8,'dp'=8,'pipe'=4] {'expert'}, dimensions={0} | all-to-all | bytes 786432 | tf_op jit(solution)/shard_map/all_to_all | solution.py:324
  25.4 2.8 collective-permute-start
  29.8 2.9 collective-permute-done.refs_1_
  32.7 2.4 collective-permute-done.1.refs_2_
  35.1 5.7 %collective-permute-done.2.refs_3_ = bf16[256,384]{1,0:T(8,128)(2,1)S(1)} collective-permute-done((bf16[256,384]{1,0:T(8,128)(2,1)S(1)}, bf16[256,384]{1,0:T(8,128)(2,1)S(1)}, u32[]{:S(2)}, u32[]{:S(2)}) %collective-permute-start.2) | collective-permute-done | bytes 196640 | tf_op jit(solution)/shard_map/ppermute | solution.py:237
  41.4 25.6 %place.2 = bf16[4,256,384]{2,1,0:T(8,128)(2,1)} custom-call(s32[4]{0:T(128)} %and_select_fusion.1.at_ref.order_ref, bf16[256,384]{1,0:T(8,128)(2,1)} %copy-done.6, bf16[256,384]{1,0:T(8,128)(2,1)} %copy-done.13, bf16[256,384]{1,0:T(8,128)(2,1)} %copy-done.14, bf16[256,384]{1,0:T(8,128)(2,1)} %copy-done.15), custom_call_target="tpu_custom_call" | custom-call | tf_op jit(solution)/shard_map/place/pallas_call | solution.py:259
  67.2 1.7 collective-permute-start.6
  68.9 4.0 %collective-permute-start.3 = (bf16[272,384]{1,0:T(8,128)(2,1)S(1)}, bf16[272,384]{1,0:T(8,128)(2,1)S(1)}, u32[]{:S(2)}, u32[]{:S(2)}) collective-permute-start(bf16[272,384]{1,0:T(8,128)(2,1)S(1)} %fusion.1.refs_0_), channel_id=1, source_target_pairs={{0,28},{4,0},{8,4},{12,8},{16,12},{20,16},{24,20},{28,24},{1,29},{... | collective-permute-start | bytes 626696 | tf_op jit(solution)/shard_map/ppermute | solution.py:237
  72.9 5.0 %collective-permute-done.6.refs_6_ = bf16[272,384]{1,0:T(8,128)(2,1)S(1)} collective-permute-done((bf16[272,384]{1,0:T(8,128)(2,1)S(1)}, bf16[272,384]{1,0:T(8,128)(2,1)S(1)}, u32[]{:S(2)}, u32[]{:S(2)}) %collective-permute-start.6) | collective-permute-done | bytes 208928 | tf_op jit(solution)/shard_map/ppermute | solution.py:237
  77.9 2.7 collective-permute-start.4
  80.6 9.6 %collective-permute-done.7.refs_5_ = bf16[272,384]{1,0:T(8,128)(2,1)S(1)} collective-permute-done((bf16[272,384]{1,0:T(8,128)(2,1)S(1)}, bf16[272,384]{1,0:T(8,128)(2,1)S(1)}, u32[]{:S(2)}, u32[]{:S(2)}) %collective-permute-start.7) | collective-permute-done | bytes 208928 | tf_op jit(solution)/shard_map/ppermute | solution.py:237
  90.2 2.7 collective-permute-start.5
  92.9 9.7 %collective-permute-done.8.refs_4_ = bf16[272,384]{1,0:T(8,128)(2,1)S(1)} collective-permute-done((bf16[272,384]{1,0:T(8,128)(2,1)S(1)}, bf16[272,384]{1,0:T(8,128)(2,1)S(1)}, u32[]{:S(2)}, u32[]{:S(2)}) %collective-permute-start.8) | collective-permute-done | bytes 208928 | tf_op jit(solution)/shard_map/ppermute | solution.py:237
  102.7 2.7 collective-permute-start.10
  106.0 3.2 collective-permute-done.10.refs_8_
  109.2 1.3 collective-permute-done.9.refs_7_
  111.3 50.6 %place.3 = (bf16[8,256,384]{2,1,0:T(8,128)(2,1)}, bf16[8,16,128]{2,1,0:T(8,128)(2,1)}) custom-call(s32[8]{0:T(128)} %and_select_fusion.at_ref, bf16[272,384]{1,0:T(8,128)(2,1)} %copy-done.5, bf16[272,384]{1,0:T(8,128)(2,1)} %copy-done.10, bf16[272,384]{1,0:T(8,128)(2,1)} %copy-done.12, bf16[272,384]{1,0:T(8,128)(2,1)} %copy-done.8, ...), custom_call_target="tpu_custom_call" | custom-call | tf_op jit(solution)/shard_map/place/pallas_call | solution.py:259
  161.9 2.7 collective-permute-start.12
  164.6 31.3 %collective-permute-done.11.b1_ref = bf16[8,256,384]{2,1,0:T(8,128)(2,1)S(1)} collective-permute-done((bf16[8,256,384]{2,1,0:T(8,128)(2,1)}, bf16[8,256,384]{2,1,0:T(8,128)(2,1)S(1)}, u32[]{:S(2)}, u32[]{:S(2)}) %collective-permute-start.11) | collective-permute-done | bytes 1572896 | tf_op jit(solution)/shard_map/ppermute | solution.py:237
  197.1 2.0 collective-permute-start.14
  199.1 13.3 %collective-permute-done.13.b2x_ref = bf16[4,256,384]{2,1,0:T(8,128)(2,1)} collective-permute-done((bf16[4,256,384]{2,1,0:T(8,128)(2,1)S(1)}, bf16[4,256,384]{2,1,0:T(8,128)(2,1)}, u32[]{:S(2)}, u32[]{:S(2)}) %collective-permute-start.13) | collective-permute-done | bytes 786464 | tf_op jit(solution)/shard_map/ppermute | solution.py:237
  212.5 20.2 %expert.1 = (bf16[256,1024]{1,0:T(8,128)(2,1)}, bf16[256,1024]{1,0:T(8,128)(2,1)}, bf16[256,1024]{1,0:T(8,128)(2,1)}, bf16[4,8,128,384]{3,2,1,0:T(8,128)(2,1)}, bf16[8,4,128,384]{3,2,1,0:T(8,128)(2,1)}) custom-call(s32[4]{0:T(128)} %and_select_fusion.1.at_ref.order_ref, bf16[8,4,256,384]{3,2,1,0:T(8,128)(2,1)} %bitcast.27, ...), custom_call_target="tpu_custom_call" | custom-call | tf_op jit(solution)/shard_map/expert/pallas_call | solution.py:95
  232.7 8.6 %all-to-all-start.2 = ((bf16[8,4,128,384]{3,2,1,0:T(8,128)(2,1)}), bf16[8,4,128,384]{3,2,1,0:T(8,128)(2,1)S(1)}, u32[]{:S(2)}, u32[]{:S(2)}) async-start(bf16[8,4,128,384]{3,2,1,0:T(8,128)(2,1)} %get-tuple-element.19), calls=%async_computation.3 | async-start | bytes 6291456 | tf_op jit(solution)/shard_map/all_to_all | solution.py:340
  241.4 14.4 %weights.1 = (bf16[3072,256]{1,0:T(8,128)(2,1)}, bf16[3072,256]{1,0:T(8,128)(2,1)}, bf16[256,3072]{1,0:T(8,128)(2,1)}) custom-call(s32[4]{0:T(128)} %and_select_fusion.1.at_ref.order_ref, bf16[8,4,256,384]{3,2,1,0:T(8,128)(2,1)} %bitcast.28, bf16[8,256,384]{2,1,0:T(8,128)(2,1)} %get-tuple-element.16.b0_ref, bf16[8,256,384]{2,1,0:T(8,128)(2,1)} %copy-done.2, ...), custom_call_target="tpu_custom_call" | custom-call | tf_op jit(solution)/shard_map/weights/pallas_call | solution.py:165
  255.8 23.0 %all-to-all-done.2.x_ref = bf16[8,4,128,384]{3,2,1,0:T(8,128)(2,1)S(1)} async-done(((bf16[8,4,128,384]{3,2,1,0:T(8,128)(2,1)}), bf16[8,4,128,384]{3,2,1,0:T(8,128)(2,1)S(1)}, u32[]{:S(2)}, u32[]{:S(2)}) %all-to-all-start.2) | async-done | bytes 3145760 | tf_op jit(solution)/shard_map/all_to_all | solution.py:340
  278.8 1.6 copy-done.1
  280.5 4.3 %combine.3 = bf16[4,256,384]{2,1,0:T(8,128)(2,1)} custom-call(bf16[8,4,128,384]{3,2,1,0:T(8,128)(2,1)} %copy-done.1, bf16[8,16,128]{2,1,0:T(8,128)(2,1)} %get-tuple-element.18.slots_ref), custom_call_target="tpu_custom_call" | custom-call | tf_op jit(solution)/shard_map/combine/pallas_call | solution.py:213
  284.7 15.2 %all_to_all.26 = bf16[4,256,384]{2,1,0:T(8,128)(2,1)S(1)} all-to-all(bf16[4,256,384]{2,1,0:T(8,128)(2,1)} %combine.3), channel_id=1, replica_groups=mesh['expert'=8,'dp'=8,'pipe'=4] {'pipe'}, dimensions={0} | all-to-all | bytes 1572864 | tf_op jit(solution)/shard_map/all_to_all | solution.py:344
  300.0 5.5 %all-to-all-start.1 = ((bf16[8,1,128,384]{3,2,1,0:T(8,128)(2,1)}), bf16[8,1,128,384]{3,2,1,0:T(8,128)(2,1)S(1)}, u32[]{:S(2)}, u32[]{:S(2)}) async-start(bf16[8,1,128,384]{3,2,1,0:T(8,128)(2,1)} %bitcast.35), calls=%async_computation.2 | async-start | bytes 1572864 | tf_op jit(solution)/shard_map/all_to_all | solution.py:346
  305.6 12.1 %all-to-all-done.1.x_ref = bf16[8,1,128,384]{3,2,1,0:T(8,128)(2,1)S(1)} async-done(((bf16[8,1,128,384]{3,2,1,0:T(8,128)(2,1)}), bf16[8,1,128,384]{3,2,1,0:T(8,128)(2,1)S(1)}, u32[]{:S(2)}, u32[]{:S(2)}) %all-to-all-start.1) | async-done | bytes 786464 | tf_op jit(solution)/shard_map/all_to_all | solution.py:346
  318.6 2.1 combine.2
  321.7 18.6 %all_to_all.27 = bf16[8,32,768]{2,1,0:T(8,128)(2,1)S(1)} all-to-all(bf16[8,32,768]{2,1,0:T(8,128)(2,1)S(1)} %pad_maximum_fusion.1), channel_id=1, replica_groups=mesh['expert'=8,'dp'=8,'pipe'=4] {'dp'}, dimensions={0} | all-to-all | bytes 786432 | tf_op jit(solution)/shard_map/all_to_all | solution.py:351
  (78 shorter events, 12.1 us)
Async XLA Ops:
  7.2 3.0 copy-start
  7.2 205.3 %all-gather.3.cloned.1.call-start = ((), (), s32[]{:S(2)}) async-start(), calls=%async_computation.7 | async-start | bytes 7077888 | tf_op jit(solution)/shard_map/all_gather | solution.py:331
  25.4 15.4 %copy-start.6 = (bf16[256,384]{1,0:T(8,128)(2,1)}, bf16[256,384]{1,0:T(8,128)(2,1)S(1)}, u32[]{:S(2)}) copy-start(bf16[256,384]{1,0:T(8,128)(2,1)S(1)} %get-tuple-element.31.refs_0_) | copy-start | bytes 589828
  25.4 7.3 %collective-permute-start = (bf16[256,384]{1,0:T(8,128)(2,1)S(1)}, bf16[256,384]{1,0:T(8,128)(2,1)S(1)}, u32[]{:S(2)}, u32[]{:S(2)}) collective-permute-start(bf16[256,384]{1,0:T(8,128)(2,1)S(1)} %get-tuple-element.31.refs_0_), channel_id=1, source_target_pairs={{0,3},{1,0},{2,1},{3,2},{4,7},{5,4},{6,5},{7,6},{8,11},{9,8},{10,9... | collective-permute-start | bytes 589832 | tf_op jit(solution)/shard_map/ppermute | solution.py:237
  28.2 6.9 %collective-permute-start.1 = (bf16[256,384]{1,0:T(8,128)(2,1)S(1)}, bf16[256,384]{1,0:T(8,128)(2,1)S(1)}, u32[]{:S(2)}, u32[]{:S(2)}) collective-permute-start(bf16[256,384]{1,0:T(8,128)(2,1)S(1)} %get-tuple-element.31.refs_0_), channel_id=1, source_target_pairs={{0,2},{1,3},{2,0},{3,1},{4,6},{5,7},{6,4},{7,5},{8,10},{9,11},{10,... | collective-permute-start | bytes 589832 | tf_op jit(solution)/shard_map/ppermute | solution.py:237
  28.6 12.2 %collective-permute-start.2 = (bf16[256,384]{1,0:T(8,128)(2,1)S(1)}, bf16[256,384]{1,0:T(8,128)(2,1)S(1)}, u32[]{:S(2)}, u32[]{:S(2)}) collective-permute-start(bf16[256,384]{1,0:T(8,128)(2,1)S(1)} %get-tuple-element.31.refs_0_), channel_id=1, source_target_pairs={{0,1},{1,2},{2,3},{3,0},{4,5},{5,6},{6,7},{7,4},{8,9},{9,10},{10,1... | collective-permute-start | bytes 589832 | tf_op jit(solution)/shard_map/ppermute | solution.py:237
  32.7 8.1 %copy-start.13 = (bf16[256,384]{1,0:T(8,128)(2,1)}, bf16[256,384]{1,0:T(8,128)(2,1)S(1)}, u32[]{:S(2)}) copy-start(bf16[256,384]{1,0:T(8,128)(2,1)S(1)} %collective-permute-done.refs_1_) | copy-start | bytes 589828
  35.1 5.7 %copy-start.14 = (bf16[256,384]{1,0:T(8,128)(2,1)}, bf16[256,384]{1,0:T(8,128)(2,1)S(1)}, u32[]{:S(2)}) copy-start(bf16[256,384]{1,0:T(8,128)(2,1)S(1)} %collective-permute-done.1.refs_2_) | copy-start | bytes 589828
  67.1 232.9 %reduce-scatter.2.cloned.1.call-start = ((), (), s32[]{:S(2)}) async-start(), calls=%async_computation.6 | async-start | bytes 3932160 | tf_op jit(solution)/shard_map/reduce_scatter | solution.py:337
  67.2 43.4 %copy-start.5 = (bf16[272,384]{1,0:T(8,128)(2,1)}, bf16[272,384]{1,0:T(8,128)(2,1)S(1)}, u32[]{:S(2)}) copy-start(bf16[272,384]{1,0:T(8,128)(2,1)S(1)} %fusion.1.refs_0_) | copy-start | bytes 626692
  67.2 10.7 %collective-permute-start.6 = (bf16[272,384]{1,0:T(8,128)(2,1)S(1)}, bf16[272,384]{1,0:T(8,128)(2,1)S(1)}, u32[]{:S(2)}, u32[]{:S(2)}) collective-permute-start(bf16[272,384]{1,0:T(8,128)(2,1)S(1)} %fusion.1.refs_0_), channel_id=1, source_target_pairs={{0,4},{4,8},{8,12},{12,16},{16,20},{20,24},{24,28},{28,0},{1,5},{5... | collective-permute-start | bytes 626696 | tf_op jit(solution)/shard_map/ppermute | solution.py:237
  68.9 9.0 %collective-permute-start.3 = (bf16[272,384]{1,0:T(8,128)(2,1)S(1)}, bf16[272,384]{1,0:T(8,128)(2,1)S(1)}, u32[]{:S(2)}, u32[]{:S(2)}) collective-permute-start(bf16[272,384]{1,0:T(8,128)(2,1)S(1)} %fusion.1.refs_0_), channel_id=1, source_target_pairs={{0,28},{4,0},{8,4},{12,8},{16,12},{20,16},{24,20},{28,24},{1,29},{... | collective-permute-start | bytes 626696 | tf_op jit(solution)/shard_map/ppermute | solution.py:237
  77.9 32.7 %copy-start.9 = (bf16[272,384]{1,0:T(8,128)(2,1)}, bf16[272,384]{1,0:T(8,128)(2,1)S(1)}, u32[]{:S(2)}) copy-start(bf16[272,384]{1,0:T(8,128)(2,1)S(1)} %collective-permute-done.6.refs_6_) | copy-start | bytes 626692
  77.9 12.3 %collective-permute-start.7 = (bf16[272,384]{1,0:T(8,128)(2,1)S(1)}, bf16[272,384]{1,0:T(8,128)(2,1)S(1)}, u32[]{:S(2)}, u32[]{:S(2)}) collective-permute-start(bf16[272,384]{1,0:T(8,128)(2,1)S(1)} %collective-permute-done.6.refs_6_), channel_id=1, source_target_pairs={{0,4},{4,8},{8,12},{12,16},{16,20},{20,24},{24,28},{28,0},{1,5},{5... | collective-permute-start | bytes 626696 | tf_op jit(solution)/shard_map/ppermute | solution.py:237
  77.9 32.6 %copy-start.10 = (bf16[272,384]{1,0:T(8,128)(2,1)}, bf16[272,384]{1,0:T(8,128)(2,1)S(1)}, u32[]{:S(2)}) copy-start(bf16[272,384]{1,0:T(8,128)(2,1)S(1)} %collective-permute-done.3.refs_1_) | copy-start | bytes 626692
  77.9 12.3 %collective-permute-start.4 = (bf16[272,384]{1,0:T(8,128)(2,1)S(1)}, bf16[272,384]{1,0:T(8,128)(2,1)S(1)}, u32[]{:S(2)}, u32[]{:S(2)}) collective-permute-start(bf16[272,384]{1,0:T(8,128)(2,1)S(1)} %collective-permute-done.3.refs_1_), channel_id=1, source_target_pairs={{0,28},{4,0},{8,4},{12,8},{16,12},{20,16},{24,20},{28,24},{1,29},{... | collective-permute-start | bytes 626696 | tf_op jit(solution)/shard_map/ppermute | solution.py:237
  90.2 20.4 %copy-start.11 = (bf16[272,384]{1,0:T(8,128)(2,1)}, bf16[272,384]{1,0:T(8,128)(2,1)S(1)}, u32[]{:S(2)}) copy-start(bf16[272,384]{1,0:T(8,128)(2,1)S(1)} %collective-permute-done.7.refs_5_) | copy-start | bytes 626692
  90.2 12.3 %collective-permute-start.8 = (bf16[272,384]{1,0:T(8,128)(2,1)S(1)}, bf16[272,384]{1,0:T(8,128)(2,1)S(1)}, u32[]{:S(2)}, u32[]{:S(2)}) collective-permute-start(bf16[272,384]{1,0:T(8,128)(2,1)S(1)} %collective-permute-done.7.refs_5_), channel_id=1, source_target_pairs={{0,4},{4,8},{8,12},{12,16},{16,20},{20,24},{24,28},{28,0},{1,5},{5... | collective-permute-start | bytes 626696 | tf_op jit(solution)/shard_map/ppermute | solution.py:237
  90.2 20.4 %copy-start.12 = (bf16[272,384]{1,0:T(8,128)(2,1)}, bf16[272,384]{1,0:T(8,128)(2,1)S(1)}, u32[]{:S(2)}) copy-start(bf16[272,384]{1,0:T(8,128)(2,1)S(1)} %collective-permute-done.4.refs_2_) | copy-start | bytes 626692
  90.2 12.4 %collective-permute-start.5 = (bf16[272,384]{1,0:T(8,128)(2,1)S(1)}, bf16[272,384]{1,0:T(8,128)(2,1)S(1)}, u32[]{:S(2)}, u32[]{:S(2)}) collective-permute-start(bf16[272,384]{1,0:T(8,128)(2,1)S(1)} %collective-permute-done.4.refs_2_), channel_id=1, source_target_pairs={{0,28},{4,0},{8,4},{12,8},{16,12},{20,16},{24,20},{28,24},{1,29},{... | collective-permute-start | bytes 626696 | tf_op jit(solution)/shard_map/ppermute | solution.py:237
  102.5 8.0 %copy-start.7 = (bf16[272,384]{1,0:T(8,128)(2,1)}, bf16[272,384]{1,0:T(8,128)(2,1)S(1)}, u32[]{:S(2)}) copy-start(bf16[272,384]{1,0:T(8,128)(2,1)S(1)} %collective-permute-done.8.refs_4_) | copy-start | bytes 626692
  102.6 8.0 %collective-permute-start.9 = (bf16[144,384]{1,0:T(8,128)(2,1)S(1)}, bf16[144,384]{1,0:T(8,128)(2,1)S(1)}, u32[]{:S(2)}, u32[]{:S(2)}) collective-permute-start(bf16[144,384]{1,0:T(8,128)(2,1)S(1)} %slice.74), channel_id=1, source_target_pairs={{0,4},{4,8},{8,12},{12,16},{16,20},{20,24},{24,28},{28,0},{1,5},{5... | collective-permute-start | bytes 331784 | tf_op jit(solution)/shard_map/ppermute | solution.py:237
  102.7 7.9 %copy-start.8 = (bf16[272,384]{1,0:T(8,128)(2,1)}, bf16[272,384]{1,0:T(8,128)(2,1)S(1)}, u32[]{:S(2)}) copy-start(bf16[272,384]{1,0:T(8,128)(2,1)S(1)} %collective-permute-done.5.refs_3_) | copy-start | bytes 626692
  102.7 6.5 %collective-permute-start.10 = (bf16[128,384]{1,0:T(8,128)(2,1)S(1)}, bf16[128,384]{1,0:T(8,128)(2,1)S(1)}, u32[]{:S(2)}, u32[]{:S(2)}) collective-permute-start(bf16[128,384]{1,0:T(8,128)(2,1)S(1)} %slice.75), channel_id=1, source_target_pairs={{0,28},{4,0},{8,4},{12,8},{16,12},{20,16},{24,20},{28,24},{1,29},{... | collective-permute-start | bytes 294920 | tf_op jit(solution)/shard_map/ppermute | solution.py:237
  161.8 34.1 %collective-permute-start.11 = (bf16[8,256,384]{2,1,0:T(8,128)(2,1)}, bf16[8,256,384]{2,1,0:T(8,128)(2,1)S(1)}, u32[]{:S(2)}, u32[]{:S(2)}) collective-permute-start(bf16[8,256,384]{2,1,0:T(8,128)(2,1)} %get-tuple-element.16.b0_ref), channel_id=1, source_target_pairs={{0,1},{1,2},{2,3},{3,0},{4,5},{5,6},{6,7},{7,4},{8,9},{9,10},{10,1... | collective-permute-start | bytes 4718600 | tf_op jit(solution)/shard_map/ppermute | solution.py:237
  161.9 34.4 %collective-permute-start.12 = (bf16[8,256,384]{2,1,0:T(8,128)(2,1)}, bf16[8,256,384]{2,1,0:T(8,128)(2,1)S(1)}, u32[]{:S(2)}, u32[]{:S(2)}) collective-permute-start(bf16[8,256,384]{2,1,0:T(8,128)(2,1)} %get-tuple-element.16.b0_ref), channel_id=1, source_target_pairs={{0,3},{1,0},{2,1},{3,2},{4,7},{5,4},{6,5},{7,6},{8,11},{9,8},{10,9... | collective-permute-start | bytes 4718600 | tf_op jit(solution)/shard_map/ppermute | solution.py:237
  196.0 16.5 %collective-permute-start.13 = (bf16[4,256,384]{2,1,0:T(8,128)(2,1)S(1)}, bf16[4,256,384]{2,1,0:T(8,128)(2,1)}, u32[]{:S(2)}, u32[]{:S(2)}) collective-permute-start(bf16[4,256,384]{2,1,0:T(8,128)(2,1)S(1)} %slice.76), channel_id=1, source_target_pairs={{0,1},{1,2},{2,3},{3,0},{4,5},{5,6},{6,7},{7,4},{8,9},{9,10},{10,1... | collective-permute-start | bytes 2359304 | tf_op jit(solution)/shard_map/ppermute | solution.py:237
  196.3 16.2 %copy-start.3 = (bf16[8,256,384]{2,1,0:T(8,128)(2,1)}, bf16[8,256,384]{2,1,0:T(8,128)(2,1)S(1)}, u32[]{:S(2)}) copy-start(bf16[8,256,384]{2,1,0:T(8,128)(2,1)S(1)} %collective-permute-done.12.b3_ref) | copy-start | bytes 4718596
  197.1 15.4 %collective-permute-start.14 = (bf16[4,256,384]{2,1,0:T(8,128)(2,1)S(1)}, bf16[4,256,384]{2,1,0:T(8,128)(2,1)}, u32[]{:S(2)}, u32[]{:S(2)}) collective-permute-start(bf16[4,256,384]{2,1,0:T(8,128)(2,1)S(1)} %slice.77), channel_id=1, source_target_pairs={{0,3},{1,0},{2,1},{3,2},{4,7},{5,4},{6,5},{7,6},{8,11},{9,8},{10,9... | collective-permute-start | bytes 2359304 | tf_op jit(solution)/shard_map/ppermute | solution.py:237
  232.7 46.1 %all-to-all-start.2 = ((bf16[8,4,128,384]{3,2,1,0:T(8,128)(2,1)}), bf16[8,4,128,384]{3,2,1,0:T(8,128)(2,1)S(1)}, u32[]{:S(2)}, u32[]{:S(2)}) async-start(bf16[8,4,128,384]{3,2,1,0:T(8,128)(2,1)} %get-tuple-element.19), calls=%async_computation.3 | async-start | bytes 6291456 | tf_op jit(solution)/shard_map/all_to_all | solution.py:340
  278.8 1.6 copy-start.1
  300.0 17.7 %all-to-all-start.1 = ((bf16[8,1,128,384]{3,2,1,0:T(8,128)(2,1)}), bf16[8,1,128,384]{3,2,1,0:T(8,128)(2,1)S(1)}, u32[]{:S(2)}, u32[]{:S(2)}) async-start(bf16[8,1,128,384]{3,2,1,0:T(8,128)(2,1)} %bitcast.35), calls=%async_computation.2 | async-start | bytes 1572864 | tf_op jit(solution)/shard_map/all_to_all | solution.py:346
  (5 other events, 4.8 us)
Sparse Core Ops, SparseCore 0:
  67.2 84.0 all-gather.2
  232.8 42.7 reduce-scatter.1
